TPU v7x, 256 devices: a whole 4x4x8 slice. The times are simulated.
256 devices in a mesh: shot: 8 (over x, y_lo), domain: 32 (over z, y_hi, core).
Axes of the slice: x: 4, y: 4 (y_hi: 2, y_lo: 2; y = y_hi * 2 + y_lo), z: 8, core: 2. Of those that a mesh axis runs over, the one named last changes fastest.
Arguments:
- velsq: float32 [64, 256, 128], P('domain', 'shot'), may hold values from 0.04 to 0.12
- epsilon: float32 [64, 256, 128], P('domain', 'shot'), may hold values from 0 to 0.3
- delta: float32 [64, 256, 128], P('domain', 'shot'), may hold values from 0 to 0.15
- tilt: float32 [64, 256, 128], P('domain', 'shot'), may hold values from -1.2 to 1.2
- azimuth: float32 [64, 256, 128], P('domain', 'shot'), may hold values from -3.140625 to 3.140625
- forward_state: float32 [8, 4, 64, 256, 128], P('shot', None, 'domain'), may hold values from -6 to 6
- adjoint_state: float32 [8, 4, 64, 256, 128], P('shot', None, 'domain'), may hold values from -6 to 6
- wavelet: float32 [8, 2], P('shot'), may hold values from -60 to 60
- source: int32 [8], P('shot'), may hold values from 0 to 2097151
- receivers: int32 [8, 256], P('shot'), may hold values from 0 to 2097151
- observed: float32 [8, 2, 256], P('shot'), may hold values from -18 to 18
Outputs:
- gradients: float32 [5, 64, 256, 128], P(None, 'domain', 'shot')
Inputs may be any that keep to these rules, and one draw needn't show every extreme that they name: `source`: flat index x * 256 * 128 + y * 128 + z of a grid cell. `receivers`: flat index x * 256 * 128 + y * 128 + z of a grid cell; cells may repeat.
All inputs are finite; a program needn't handle non-finite values.
Results may differ from a plain program's by a relative error of at most 0.0001.
Values sent between devices are 32-bit elements; how exact they have to be, the bound alone decides.
A program may use at most 128 MiB of HBM per device.

v0:
```python
import jax
import jax.numpy as jnp
from jax import lax
from jax.sharding import PartitionSpec as P

STEPS = 2


def with_halo(block, sides, width):
    for axis, dim in sides:
        count = lax.axis_size(axis)
        forward = [(i, i + 1) for i in range(count - 1)]
        backward = [(target, source) for source, target in forward]
        low = lax.ppermute(
            lax.slice_in_dim(block, block.shape[dim] - width, None, axis=dim), axis, forward
        )
        high = lax.ppermute(lax.slice_in_dim(block, 0, width, axis=dim), axis, backward)
        block = jnp.concatenate([low, block, high], axis=dim)
    return block


def hessian(values):
    padded = jnp.pad(values, ((0, 0), (1, 1), (1, 1)))
    center = padded[1:-1, 1:-1, 1:-1]
    curve_xx = padded[2:, 1:-1, 1:-1] + padded[:-2, 1:-1, 1:-1] - 2.0 * center
    curve_yy = padded[1:-1, 2:, 1:-1] + padded[1:-1, :-2, 1:-1] - 2.0 * center
    curve_zz = padded[1:-1, 1:-1, 2:] + padded[1:-1, 1:-1, :-2] - 2.0 * center
    mixed_xy = 0.25 * (
        padded[2:, 2:, 1:-1]
        - padded[2:, :-2, 1:-1]
        - padded[:-2, 2:, 1:-1]
        + padded[:-2, :-2, 1:-1]
    )
    mixed_xz = 0.25 * (
        padded[2:, 1:-1, 2:]
        - padded[2:, 1:-1, :-2]
        - padded[:-2, 1:-1, 2:]
        + padded[:-2, 1:-1, :-2]
    )
    mixed_yz = 0.25 * (
        padded[1:-1, 2:, 2:]
        - padded[1:-1, 2:, :-2]
        - padded[1:-1, :-2, 2:]
        + padded[1:-1, :-2, :-2]
    )
    return jnp.stack([curve_xx, curve_yy, curve_zz, mixed_xy, mixed_xz, mixed_yz])


def tables(velsq, epsilon, delta, tilt, azimuth):
    sin_tilt = jnp.sin(tilt)
    cos_tilt = jnp.cos(tilt)
    sin_azim = jnp.sin(azimuth)
    cos_azim = jnp.cos(azimuth)
    axis_x = sin_tilt * cos_azim
    axis_y = sin_tilt * sin_azim
    turn_x = cos_tilt * cos_azim
    turn_y = cos_tilt * sin_azim
    turn_z = -sin_tilt
    spin_x = -sin_tilt * sin_azim
    spin_y = sin_tilt * cos_azim
    along = jnp.stack(
        [
            axis_x * axis_x,
            axis_y * axis_y,
            cos_tilt * cos_tilt,
            2.0 * axis_x * axis_y,
            2.0 * axis_x * cos_tilt,
            2.0 * axis_y * cos_tilt,
        ]
    )
    by_tilt = jnp.stack(
        [
            2.0 * turn_x * axis_x,
            2.0 * turn_y * axis_y,
            2.0 * turn_z * cos_tilt,
            2.0 * (turn_x * axis_y + turn_y * axis_x),
            2.0 * (turn_x * cos_tilt + turn_z * axis_x),
            2.0 * (turn_y * cos_tilt + turn_z * axis_y),
        ]
    )
    by_spin = jnp.stack(
        [
            2.0 * spin_x * axis_x,
            2.0 * spin_y * axis_y,
            jnp.zeros_like(cos_tilt),
            2.0 * (spin_x * axis_y + spin_y * axis_x),
            2.0 * spin_x * cos_tilt,
            2.0 * spin_y * cos_tilt,
        ]
    )
    return (velsq, 1.0 + 2.0 * epsilon, jnp.sqrt(1.0 + 2.0 * delta), along, by_tilt, by_spin)


def operate(pad_p, pad_q, table, full):
    speed_sq, stretch, root_d, along, by_tilt, by_spin = table
    hess_p = hessian(pad_p)
    hess_q = hessian(pad_q)
    laplace = hess_p[0] + hess_p[1] + hess_p[2]
    axial_p = jnp.sum(along * hess_p, axis=0)
    axial_q = jnp.sum(along * hess_q, axis=0)
    across = laplace - axial_p
    drive_p = stretch * across + root_d * axial_q
    drive_q = root_d * across + axial_q
    if full:
        image_terms = (
            across,
            axial_q,
            jnp.sum(by_tilt * hess_p, axis=0),
            jnp.sum(by_tilt * hess_q, axis=0),
            jnp.sum(by_spin * hess_p, axis=0),
            jnp.sum(by_spin * hess_q, axis=0),
        )
        return (drive_p, drive_q, image_terms)
    return (drive_p, drive_q, ())


def advance(pad_p, pad_q, prior_p, prior_q, table, full):
    drive_p, drive_q, image_terms = operate(pad_p, pad_q, table, full)
    speed_sq = table[0]
    next_p = 2.0 * pad_p[1:-1] - prior_p + speed_sq * drive_p
    next_q = 2.0 * pad_q[1:-1] - prior_q + speed_sq * drive_q
    return (next_p, next_q, image_terms)


def correlate(gradient, adjoint_p, adjoint_q, image_terms, table):
    speed_sq, stretch, root_d, along, by_tilt, by_spin = table
    across, axial_q, tilt_p, tilt_q, spin_p, spin_q = image_terms
    g_speed = (
        gradient[0]
        + adjoint_p * (stretch * across + root_d * axial_q)
        + adjoint_q * (root_d * across + axial_q)
    )
    g_eps = gradient[1] + 2.0 * speed_sq * adjoint_p * across
    g_delta = gradient[2] + speed_sq * (adjoint_p * axial_q + adjoint_q * across) / root_d
    g_tilt = gradient[3] + speed_sq * (
        adjoint_p * (root_d * tilt_q - stretch * tilt_p) + adjoint_q * (tilt_q - root_d * tilt_p)
    )
    g_spin = gradient[4] + speed_sq * (
        adjoint_p * (root_d * spin_q - stretch * spin_p) + adjoint_q * (spin_q - root_d * spin_p)
    )
    return (g_speed, g_eps, g_delta, g_tilt, g_spin)


def inject(values, start_row, target, amount):
    layout = values.shape
    plane_size = layout[1] * layout[2]
    offset = target - start_row * plane_size
    inside = (offset >= 0) & (offset < layout[0] * plane_size)
    clipped = jnp.where(inside, offset, 0)
    return values.reshape(-1).at[clipped].add(jnp.where(inside, amount, 0.0)).reshape(layout)


def sample_cells(values, start_row, target):
    layout = values.shape
    plane_size = layout[1] * layout[2]
    offset = target - start_row * plane_size
    inside = (offset >= 0) & (offset < layout[0] * plane_size)
    clipped = jnp.where(inside, offset, 0)
    return jnp.where(inside, values.reshape(-1)[clipped], 0.0)


def single_rim(field_p, field_q):
    padded = with_halo(jnp.stack([field_p, field_q]), (("domain", 1),), 1)
    return (padded[0], padded[1])


def shards(
    velsq,
    epsilon,
    delta,
    tilt,
    azimuth,
    forward_state,
    adjoint_state,
    wavelet,
    source,
    receivers,
    observed,
):
    gathered = (
        lax.all_gather(velsq, "shot", axis=1, tiled=True),
        lax.all_gather(epsilon, "shot", axis=1, tiled=True),
        lax.all_gather(delta, "shot", axis=1, tiled=True),
        lax.all_gather(tilt, "shot", axis=1, tiled=True),
        lax.all_gather(azimuth, "shot", axis=1, tiled=True),
    )
    row_count = gathered[0].shape[0]
    first_row = lax.axis_index("domain") * row_count
    inner = tables(gathered[0], gathered[1], gathered[2], gathered[3], gathered[4])
    full_terms = False
    full_terms = True
    source_cell = source[0]
    receiver_cells = receivers[0]
    older_p, field_p, older_q, field_q = (
        forward_state[0, 0],
        forward_state[0, 1],
        forward_state[0, 2],
        forward_state[0, 3],
    )
    saved = []
    traces = []
    for moment in range(STEPS):
        pad_p, pad_q = single_rim(field_p, field_q)
        next_p, next_q, image_terms = advance(pad_p, pad_q, older_p, older_q, inner, full_terms)
        next_p = inject(next_p, first_row, source_cell, wavelet[0, moment])
        next_q = inject(next_q, first_row, source_cell, wavelet[0, moment])
        saved.append(image_terms)
        traces.append(sample_cells(next_p, first_row, receiver_cells))
        older_p, field_p, older_q, field_q = (field_p, next_p, field_q, next_q)
    recorded = lax.psum(jnp.stack(traces), "domain")
    misfit = recorded - observed[0]
    gradient = tuple((jnp.zeros(field_p.shape, jnp.float32) for member in range(5)))
    before_p, adjoint_p, before_q, adjoint_q = (
        adjoint_state[0, 0],
        adjoint_state[0, 1],
        adjoint_state[0, 2],
        adjoint_state[0, 3],
    )
    for moment in range(STEPS):
        back_index = STEPS - 1 - moment
        gradient = correlate(gradient, adjoint_p, adjoint_q, saved[back_index], inner)
        pad_p, pad_q = single_rim(adjoint_p, adjoint_q)
        next_p, next_q, unused = advance(pad_p, pad_q, before_p, before_q, inner, False)
        next_p = inject(next_p, first_row, receiver_cells, misfit[back_index])
        before_p, adjoint_p, before_q, adjoint_q = (adjoint_p, next_p, adjoint_q, next_q)
    return lax.psum_scatter(jnp.stack(gradient), "shot", scatter_dimension=2, tiled=True)


def solution(mesh):
    placed = (
        P("domain", "shot", None),
        P("domain", "shot", None),
        P("domain", "shot", None),
        P("domain", "shot", None),
        P("domain", "shot", None),
        P("shot", None, "domain", None, None),
        P("shot", None, "domain", None, None),
        P("shot", None),
        P("shot"),
        P("shot", None),
        P("shot", None, None),
    )
    return jax.shard_map(
        shards,
        mesh=mesh,
        in_specs=placed,
        out_specs=P(None, "domain", "shot", None),
        check_vma=False,
    )
```

profile of v0, /device:TPU:16, one launch (start us, length us, event | category | flops | bytes accessed | tf_op | source)
XLA Modules:
  0.0 354.3 jit_solution(16403042310096619500)
XLA Ops:
  6.5 1.2 slice_bitcast_fusion.9
  7.7 0.7 fusion
  8.5 1.9 collective-permute-start.4
  10.4 2.4 collective-permute-start.5
  12.9 0.8 fusion.2
  13.7 4.8 %collective-permute-start = (f32[2,1,256,128]{3,2,1,0:T(8,128)}, f32[2,1,256,128]{3,2,1,0:T(8,128)}, u32[]{:S(2)}, u32[]{:S(2)}) collective-permute-start(f32[2,1,256,128]{3,2,1,0:T(8,128)} %get-tuple-element.99), channel_id=1, source_target_pairs={{1,0},{2,1},{3,2},{4,3},{5,4},{6,5},{7,6},{8,7},{9,8},{10,9},{11,1... | collective-permute-start | bytes 786440 | tf_op jit(solution)/shard_map/ppermute | solution.py:17
  18.5 2.6 collective-permute-start.1
  21.2 28.5 %all_gather.17 = f32[2,256,128]{2,1,0:T(8,128)S(1)} all-gather(f32[2,32,128]{2,1,0:T(8,128)S(1)} %copy-done.35), channel_id=1, replica_groups=mesh['shot'=8,'domain'=32] {'shot'}, dimensions={1}, use_global_device_ids=true | all-gather | bytes 294912 | tf_op jit(solution)/shard_map/all_gather | solution.py:184
  49.7 0.9 fusion.194
  50.6 28.6 %all_gather.18 = f32[2,256,128]{2,1,0:T(8,128)S(1)} all-gather(f32[2,32,128]{2,1,0:T(8,128)S(1)} %copy-done.36), channel_id=1, replica_groups=mesh['shot'=8,'domain'=32] {'shot'}, dimensions={1}, use_global_device_ids=true | all-gather | bytes 294912 | tf_op jit(solution)/shard_map/all_gather | solution.py:185
  79.2 0.9 fusion.193
  80.2 28.4 %all_gather.16 = f32[2,256,128]{2,1,0:T(8,128)S(1)} all-gather(f32[2,32,128]{2,1,0:T(8,128)S(1)} %copy-done.37), channel_id=1, replica_groups=mesh['shot'=8,'domain'=32] {'shot'}, dimensions={1}, use_global_device_ids=true | all-gather | bytes 294912 | tf_op jit(solution)/shard_map/all_gather | solution.py:181
  108.6 28.4 %all_gather.19 = f32[2,256,128]{2,1,0:T(8,128)S(1)} all-gather(f32[2,32,128]{2,1,0:T(8,128)S(1)} %copy-done.38), channel_id=1, replica_groups=mesh['shot'=8,'domain'=32] {'shot'}, dimensions={1}, use_global_device_ids=true | all-gather | bytes 294912 | tf_op jit(solution)/shard_map/all_gather | solution.py:183
  137.0 28.4 %all_gather.15 = f32[2,256,128]{2,1,0:T(8,128)S(1)} all-gather(f32[2,32,128]{2,1,0:T(8,128)S(1)} %copy-done.39), channel_id=1, replica_groups=mesh['shot'=8,'domain'=32] {'shot'}, dimensions={1}, use_global_device_ids=true | all-gather | bytes 294912 | tf_op jit(solution)/shard_map/all_gather | solution.py:182
  165.4 0.6 fusion.195
  166.0 0.8 bitcast_dynamic-update-slice_fusion.10
  166.8 0.9 bitcast_dynamic-update-slice_fusion.9
  167.7 0.9 bitcast_dynamic-update-slice_fusion.26
  168.6 1.0 bitcast_dynamic-update-slice_fusion.8
  169.5 0.9 bitcast_dynamic-update-slice_fusion.7
  170.5 0.9 bitcast_dynamic-update-slice_fusion.6
  171.4 1.0 bitcast_dynamic-update-slice_fusion.5
  174.3 0.7 bitcast_dynamic-update-slice_fusion.21
  175.1 1.1 pad_maximum_fusion.2
  176.3 1.1 copy-done
  177.5 1.9 subtract_dynamic-update-slice_fusion
  179.5 0.9 bitcast_dynamic-update-slice_fusion.14
  180.4 0.9 fusion.108
  181.6 0.3 fusion.120
  182.0 1.5 pad_maximum_fusion
  183.6 1.1 fusion.155
  184.9 1.1 fusion.28
  187.0 0.3 fusion.50
  187.6 0.3 fusion.24
  188.0 2.4 multiply_reduce_fusion.13
  190.4 1.4 fusion.177
  192.4 0.7 broadcast_multiply_fusion
  193.1 0.7 broadcast_multiply_fusion.1
  193.9 0.8 fusion.1
  194.7 1.9 collective-permute-start.2
  196.6 2.6 collective-permute-start.3
  199.2 0.8 fusion.134
  200.0 1.7 gather_fusion
  201.8 1.1 fusion.140
  202.8 1.0 fusion.146
  203.9 4.4 %collective-permute-done.3 = f32[2,1,256,128]{3,2,1,0:T(8,128)} collective-permute-done((f32[2,1,256,128]{3,2,1,0:T(8,128)}, f32[2,1,256,128]{3,2,1,0:T(8,128)}, u32[]{:S(2)}, u32[]{:S(2)}) %collective-permute-start.3) | collective-permute-done | bytes 262176 | tf_op jit(solution)/shard_map/ppermute | solution.py:14
  208.3 1.1 pad_maximum_fusion.1
  209.5 1.2 fusion.152
  211.4 0.3 fusion.98
  212.5 0.3 fusion.72
  212.8 0.5 copy-done.8
  213.4 0.5 copy-done.10
  213.8 5.6 %multiply_reduce_fusion.2 = (f32[2,256,128]{2,1,0:T(8,128)}, f32[2,256,128]{2,1,0:T(8,128)}, f32[2,256,128]{2,1,0:T(8,128)}, f32[2,256,128]{2,1,0:T(8,128)}, f32...) fusion(f32[6,2,256,128]{3,2,1,0:T(8,128)} %bitcast_dynamic-upda, ...), kind=kLoop, calls=%fused_computation.101 | loop fusion | flops 8650752 | bytes 17301504 | tf_op jit(solution)/shard_map/reduce_sum | solution.py:110
  219.4 2.2 fusion.182
  221.8 1.7 gather_fusion.1
  223.5 64.4 %psum.7 = f32[2,256]{1,0:T(2,128)S(1)} all-reduce(f32[2,256]{1,0:T(2,128)S(1)} %pad_maximum_fusion.18), channel_id=1, replica_groups=mesh['shot'=8,'domain'=32] {'domain'}, use_global_device_ids=true, to_apply=%region_6.7 | all-reduce | flops 512 | bytes 4096 | tf_op jit(solution)/shard_map/psum | solution.py:210
  287.9 2.1 fusion.160
  290.0 2.4 scatter_fusion
  292.5 2.0 bitcast_dynamic-update-slice_fusion.13
  294.5 0.8 bitcast_dynamic-update-slice_fusion.12
  295.3 0.9 bitcast_dynamic-update-slice_fusion.11
  296.6 1.0 bitcast_dynamic-update-slice_fusion.4
  297.8 1.0 bitcast_dynamic-update-slice_fusion
  298.8 48.7 %reduce-scatter.2.cloned.1.call-done = f32[5,2,32,128]{3,2,1,0:T(8,128)} async-done(((f32[5,2,256,128]{3,2,1,0:T(8,128)}), f32[5,2,32,128]{3,2,1,0:T(8,128)}) %reduce-scatter.2.cloned.1.call-update) | async-done | bytes 163856 | tf_op jit(solution)/shard_map/reduce_scatter | solution.py:226
  (118 shorter events, 5.2 us)
Async XLA Ops:
  6.5 6.3 %copy-start.1 = (f32[1,4,2,256,128]{4,3,2,1,0:T(8,128)S(1)}, f32[1,4,2,256,128]{4,3,2,1,0:T(8,128)}, u32[]{:S(2)}) copy-start(f32[1,4,2,256,128]{4,3,2,1,0:T(8,128)} %param.22) | copy-start | bytes 3145732
  6.5 340.9 %reduce-scatter.2.cloned.1.call-start = ((), (), s32[]{:S(2)}) async-start(), calls=%async_computation.1 | async-start | bytes 1474560 | tf_op jit(solution)/shard_map/reduce_scatter | solution.py:226
  7.7 167.3 %copy-start.11 = (f32[1,2,256,128]{3,2,1,0:T(8,128)}, f32[1,2,256,128]{3,2,1,0:T(8,128)S(1)}, u32[]{:S(2)}) copy-start(f32[1,2,256,128]{3,2,1,0:T(8,128)S(1)} %get-tuple-element.73) | copy-start | bytes 786436
  7.7 167.3 %copy-start.14 = (f32[1,2,256,128]{3,2,1,0:T(8,128)}, f32[1,2,256,128]{3,2,1,0:T(8,128)S(1)}, u32[]{:S(2)}) copy-start(f32[1,2,256,128]{3,2,1,0:T(8,128)S(1)} %get-tuple-element.74) | copy-start | bytes 786436
  7.7 13.5 %copy-start.35 = (f32[2,32,128]{2,1,0:T(8,128)S(1)}, f32[2,32,128]{2,1,0:T(8,128)}, u32[]{:S(2)}) copy-start(f32[2,32,128]{2,1,0:T(8,128)} %param.20) | copy-start | bytes 98308
  8.5 166.6 %collective-permute-start.4 = (f32[2,1,256,128]{3,2,1,0:T(8,128)}, f32[2,1,256,128]{3,2,1,0:T(8,128)}, u32[]{:S(2)}, u32[]{:S(2)}) collective-permute-start(f32[2,1,256,128]{3,2,1,0:T(8,128)} %get-tuple-element.91), channel_id=1, source_target_pairs={{1,0},{2,1},{3,2},{4,3},{5,4},{6,5},{7,6},{8,7},{9,8},{10,9},{11,1... | collective-permute-start | bytes 786440 | tf_op jit(solution)/shard_map/ppermute | solution.py:17
  10.4 40.3 %copy-start.36 = (f32[2,32,128]{2,1,0:T(8,128)S(1)}, f32[2,32,128]{2,1,0:T(8,128)}, u32[]{:S(2)}) copy-start(f32[2,32,128]{2,1,0:T(8,128)} %param.21) | copy-start | bytes 98308
  10.4 164.7 %collective-permute-start.5 = (f32[2,1,256,128]{3,2,1,0:T(8,128)S(1)}, f32[2,1,256,128]{3,2,1,0:T(8,128)}, u32[]{:S(2)}, u32[]{:S(2)}) collective-permute-start(f32[2,1,256,128]{3,2,1,0:T(8,128)S(1)} %get-tuple-element.92), channel_id=1, source_target_pairs={{0,1},{1,2},{2,3},{3,4},{4,5},{5,6},{6,7},{7,8},{8,9},{9,10},{10,1... | collective-permute-start | bytes 786440 | tf_op jit(solution)/shard_map/ppermute | solution.py:14
  12.9 67.3 %copy-start.5 = (f32[1,2,256,128]{3,2,1,0:T(8,128)}, f32[1,2,256,128]{3,2,1,0:T(8,128)S(1)}, u32[]{:S(2)}) copy-start(f32[1,2,256,128]{3,2,1,0:T(8,128)S(1)} %get-tuple-element.86) | copy-start | bytes 786436
  12.9 171.9 %copy-start.3 = (f32[1,2,256,128]{3,2,1,0:T(8,128)}, f32[1,2,256,128]{3,2,1,0:T(8,128)S(1)}, u32[]{:S(2)}) copy-start(f32[1,2,256,128]{3,2,1,0:T(8,128)S(1)} %get-tuple-element.85) | copy-start | bytes 786436
  12.9 67.3 %copy-start.37 = (f32[2,32,128]{2,1,0:T(8,128)S(1)}, f32[2,32,128]{2,1,0:T(8,128)}, u32[]{:S(2)}) copy-start(f32[2,32,128]{2,1,0:T(8,128)} %param.17) | copy-start | bytes 98308
  12.9 95.7 %copy-start.38 = (f32[2,32,128]{2,1,0:T(8,128)S(1)}, f32[2,32,128]{2,1,0:T(8,128)}, u32[]{:S(2)}) copy-start(f32[2,32,128]{2,1,0:T(8,128)} %param.19) | copy-start | bytes 98308
  13.7 123.3 %copy-start.39 = (f32[2,32,128]{2,1,0:T(8,128)S(1)}, f32[2,32,128]{2,1,0:T(8,128)}, u32[]{:S(2)}) copy-start(f32[2,32,128]{2,1,0:T(8,128)} %param.18) | copy-start | bytes 98308
  13.7 151.6 %copy-start.41 = (f32[1,2]{1,0:T(1,128)S(1)}, f32[1,2]{1,0:T(1,128)}, u32[]{:S(2)}) copy-start(f32[1,2]{1,0:T(1,128)} %param.24) | copy-start | bytes 28
  13.7 168.3 %collective-permute-start = (f32[2,1,256,128]{3,2,1,0:T(8,128)}, f32[2,1,256,128]{3,2,1,0:T(8,128)}, u32[]{:S(2)}, u32[]{:S(2)}) collective-permute-start(f32[2,1,256,128]{3,2,1,0:T(8,128)} %get-tuple-element.99), channel_id=1, source_target_pairs={{1,0},{2,1},{3,2},{4,3},{5,4},{6,5},{7,6},{8,7},{9,8},{10,9},{11,1... | collective-permute-start | bytes 786440 | tf_op jit(solution)/shard_map/ppermute | solution.py:17
  18.5 163.5 %collective-permute-start.1 = (f32[2,1,256,128]{3,2,1,0:T(8,128)}, f32[2,1,256,128]{3,2,1,0:T(8,128)}, u32[]{:S(2)}, u32[]{:S(2)}) collective-permute-start(f32[2,1,256,128]{3,2,1,0:T(8,128)} %get-tuple-element.100), channel_id=1, source_target_pairs={{0,1},{1,2},{2,3},{3,4},{4,5},{5,6},{6,7},{7,8},{8,9},{9,10},{10,1... | collective-permute-start | bytes 786440 | tf_op jit(solution)/shard_map/ppermute | solution.py:14
  169.5 1.8 copy-start.40
  176.2 1.2 copy-start
  176.2 1.3 copy-start.12
  176.2 1.3 copy-start.15
  180.4 1.6 copy-start.6
  182.0 1.6 copy-start.25
  183.5 1.4 copy-start.2
  187.3 3.1 copy-start.9
  188.0 2.4 copy-start.7
  188.0 2.4 copy-start.4
  190.4 1.4 copy-start.16
  191.8 2.1 copy-start.18
  194.7 9.2 %collective-permute-start.2 = (f32[2,1,256,128]{3,2,1,0:T(8,128)}, f32[2,1,256,128]{3,2,1,0:T(8,128)}, u32[]{:S(2)}, u32[]{:S(2)}) collective-permute-start(f32[2,1,256,128]{3,2,1,0:T(8,128)} %get-tuple-element.97), channel_id=1, source_target_pairs={{1,0},{2,1},{3,2},{4,3},{5,4},{6,5},{7,6},{8,7},{9,8},{10,9},{11,1... | collective-permute-start | bytes 786440 | tf_op jit(solution)/shard_map/ppermute | solution.py:17
  196.6 11.7 %collective-permute-start.3 = (f32[2,1,256,128]{3,2,1,0:T(8,128)}, f32[2,1,256,128]{3,2,1,0:T(8,128)}, u32[]{:S(2)}, u32[]{:S(2)}) collective-permute-start(f32[2,1,256,128]{3,2,1,0:T(8,128)} %get-tuple-element.98), channel_id=1, source_target_pairs={{0,1},{1,2},{2,3},{3,4},{4,5},{5,6},{6,7},{7,8},{8,9},{9,10},{10,1... | collective-permute-start | bytes 786440 | tf_op jit(solution)/shard_map/ppermute | solution.py:14
  209.4 1.2 copy-start.24
  210.7 1.0 copy-start.22
  211.4 1.4 copy-start.26
  211.8 1.6 copy-start.8
  211.8 2.0 copy-start.10
  219.4 2.2 copy-start.20
  219.4 68.5 %copy-start.42 = (f32[1,2,256]{2,1,0:T(2,128)S(1)}, f32[1,2,256]{2,1,0:T(2,128)}, u32[]{:S(2)}) copy-start(f32[1,2,256]{2,1,0:T(2,128)} %param.27) | copy-start | bytes 6148
  219.4 68.5 %copy-start.13 = (f32[1,2,256,128]{3,2,1,0:T(8,128)S(1)}, f32[1,2,256,128]{3,2,1,0:T(8,128)}, u32[]{:S(2)}) copy-start(f32[1,2,256,128]{3,2,1,0:T(8,128)} %copy-done.11) | copy-start | bytes 786436
  290.0 2.4 copy-start.17
  290.0 2.4 copy-start.19
  290.0 2.4 copy-start.21
  290.0 2.4 copy-start.23
  295.3 0.9 copy-start.31
  295.3 1.0 copy-start.32
  295.3 1.2 copy-start.33
  295.3 1.3 copy-start.34
  296.6 1.0 copy-start.27
  296.6 1.0 copy-start.28
  296.6 1.1 copy-start.29
  296.6 1.3 copy-start.30
Sparse Core Ops, SparseCore 0:
  298.9 48.4 reduce-scatter.1
where the time goes:
time: 355 us; the launch traced here: 354 us
  blocking collectives  207 us (58%)
  waiting for transfers between devices  53.1 us (15%)
  other arithmetic  51.8 us (15%)
  starting transfers between devices  16.2 us (5%)
  between operations  16 us (5%)
  local copies, waits for them, and re-layouts  10.5 us (3%)
    psum x1, blocking collectives, shards(): recorded = lax.psum(jnp.stack(traces), 'domain')  64.4 us
    reduce_scatter x1, waiting for transfers between devices, shards(): lax.psum_scatter(jnp.stack(gradient), 'shot', scatter_dimension=2, tiled=...  48.7 us
    all_gather x1, blocking collectives, shards(): lax.all_gather(azimuth, 'shot', axis=1, tiled=True)  28.6 us
    all_gather x1, blocking collectives, shards(): lax.all_gather(tilt, 'shot', axis=1, tiled=True)  28.5 us
    all_gather x1, blocking collectives, shards(): lax.all_gather(velsq, 'shot', axis=1, tiled=True)  28.4 us
    all_gather x1, blocking collectives, shards(): lax.all_gather(delta, 'shot', axis=1, tiled=True)  28.4 us
    all_gather x1, blocking collectives, shards(): lax.all_gather(epsilon, 'shot', axis=1, tiled=True)  28.4 us
    unnamed x33, other arithmetic  22 us
  transfers between devices with their start and end apart: 7, of which 2 were waited for; matrix products, arithmetic and copies ran while one was open for 6% of the time, Pallas kernels for 0%

commit v1 on v0

--- a/solution.py
+++ b/solution.py
@@ -207,7 +207,7 @@
         saved.append(image_terms)
         traces.append(sample_cells(next_p, first_row, receiver_cells))
         older_p, field_p, older_q, field_q = (field_p, next_p, field_q, next_q)
-    recorded = lax.psum(jnp.stack(traces), "domain")
+    recorded = jnp.sum(lax.all_gather(jnp.stack(traces), "domain"), axis=0)
     misfit = recorded - observed[0]
     gradient = tuple((jnp.zeros(field_p.shape, jnp.float32) for member in range(5)))
     before_p, adjoint_p, before_q, adjoint_q = (

time: 355 us -> 329 us (0.927)
  blocking collectives: 207 us -> 185 us
  waiting for transfers between devices: 53.1 us -> 48.7 us
    psum x1 -> x0, blocking collectives: 64.4 us -> none  [shards(): recorded = lax.psum(jnp.stack(traces), 'domain')]
    all_gather x0 -> x1, blocking collectives: none -> 42.5 us  [shards(): recorded = jnp.sum(lax.all_gather(jnp.stack(traces), 'domain'), axis=0)]
    reduce_scatter x1, waiting for transfers between devices: 48.7 us -> 44.3 us  [shards(): lax.psum_scatter(jnp.stack(gradient), 'shot', scatter_dimension=2, tiled=...]
    unnamed x33 -> x34, other arithmetic: 22 us -> 22.1 us
where the time goes in v1:
time: 329 us; the launch traced here: 328 us
  blocking collectives  185 us (56%)
  other arithmetic  51.8 us (16%)
  waiting for transfers between devices  48.7 us (15%)
  starting transfers between devices  16.2 us (5%)
  between operations  16 us (5%)
  local copies, waits for them, and re-layouts  10.5 us (3%)
    reduce_scatter x1, waiting for transfers between devices, shards(): lax.psum_scatter(jnp.stack(gradient), 'shot', scatter_dimension=2, tiled=...  44.3 us
    all_gather x1, blocking collectives, shards(): recorded = jnp.sum(lax.all_gather(jnp.stack(traces), 'domain'), axis=0)  42.5 us
    all_gather x1, blocking collectives, shards(): lax.all_gather(azimuth, 'shot', axis=1, tiled=True)  28.6 us
    all_gather x1, blocking collectives, shards(): lax.all_gather(tilt, 'shot', axis=1, tiled=True)  28.5 us
    all_gather x1, blocking collectives, shards(): lax.all_gather(velsq, 'shot', axis=1, tiled=True)  28.4 us
    all_gather x1, blocking collectives, shards(): lax.all_gather(delta, 'shot', axis=1, tiled=True)  28.4 us
    all_gather x1, blocking collectives, shards(): lax.all_gather(epsilon, 'shot', axis=1, tiled=True)  28.4 us
    unnamed x34, other arithmetic  22.1 us
  transfers between devices with their start and end apart: 7, of which 2 were waited for; matrix products, arithmetic and copies ran while one was open for 6% of the time, Pallas kernels for 0%

profile of v1, /device:TPU:16, one launch (start us, length us, event | category | flops | bytes accessed | tf_op | source)
XLA Modules:
  0.0 328.1 jit_solution(10833082207508529991)
XLA Ops:
  6.5 1.2 slice_bitcast_fusion.9
  7.7 0.7 fusion
  8.5 1.9 collective-permute-start.4
  10.4 2.4 collective-permute-start.5
  12.9 0.8 fusion.2
  13.7 4.8 %collective-permute-start = (f32[2,1,256,128]{3,2,1,0:T(8,128)}, f32[2,1,256,128]{3,2,1,0:T(8,128)}, u32[]{:S(2)}, u32[]{:S(2)}) collective-permute-start(f32[2,1,256,128]{3,2,1,0:T(8,128)} %get-tuple-element.99), channel_id=1, source_target_pairs={{1,0},{2,1},{3,2},{4,3},{5,4},{6,5},{7,6},{8,7},{9,8},{10,9},{11,1... | collective-permute-start | bytes 786440 | tf_op jit(solution)/shard_map/ppermute | solution.py:17
  18.5 2.6 collective-permute-start.1
  21.2 28.5 %all_gather.23 = f32[2,256,128]{2,1,0:T(8,128)S(1)} all-gather(f32[2,32,128]{2,1,0:T(8,128)S(1)} %copy-done.35), channel_id=1, replica_groups=mesh['shot'=8,'domain'=32] {'shot'}, dimensions={1}, use_global_device_ids=true | all-gather | bytes 294912 | tf_op jit(solution)/shard_map/all_gather | solution.py:184
  49.7 0.9 fusion.194
  50.6 28.6 %all_gather.24 = f32[2,256,128]{2,1,0:T(8,128)S(1)} all-gather(f32[2,32,128]{2,1,0:T(8,128)S(1)} %copy-done.36), channel_id=1, replica_groups=mesh['shot'=8,'domain'=32] {'shot'}, dimensions={1}, use_global_device_ids=true | all-gather | bytes 294912 | tf_op jit(solution)/shard_map/all_gather | solution.py:185
  79.2 0.9 fusion.193
  80.2 28.4 %all_gather.22 = f32[2,256,128]{2,1,0:T(8,128)S(1)} all-gather(f32[2,32,128]{2,1,0:T(8,128)S(1)} %copy-done.37), channel_id=1, replica_groups=mesh['shot'=8,'domain'=32] {'shot'}, dimensions={1}, use_global_device_ids=true | all-gather | bytes 294912 | tf_op jit(solution)/shard_map/all_gather | solution.py:181
  108.6 28.4 %all_gather.25 = f32[2,256,128]{2,1,0:T(8,128)S(1)} all-gather(f32[2,32,128]{2,1,0:T(8,128)S(1)} %copy-done.38), channel_id=1, replica_groups=mesh['shot'=8,'domain'=32] {'shot'}, dimensions={1}, use_global_device_ids=true | all-gather | bytes 294912 | tf_op jit(solution)/shard_map/all_gather | solution.py:183
  137.0 28.4 %all_gather.21 = f32[2,256,128]{2,1,0:T(8,128)S(1)} all-gather(f32[2,32,128]{2,1,0:T(8,128)S(1)} %copy-done.39), channel_id=1, replica_groups=mesh['shot'=8,'domain'=32] {'shot'}, dimensions={1}, use_global_device_ids=true | all-gather | bytes 294912 | tf_op jit(solution)/shard_map/all_gather | solution.py:182
  165.4 0.6 fusion.195
  166.0 0.8 bitcast_dynamic-update-slice_fusion.10
  166.8 0.9 bitcast_dynamic-update-slice_fusion.9
  167.7 0.9 bitcast_dynamic-update-slice_fusion.26
  168.6 1.0 bitcast_dynamic-update-slice_fusion.8
  169.5 0.9 bitcast_dynamic-update-slice_fusion.7
  170.5 0.9 bitcast_dynamic-update-slice_fusion.6
  171.4 1.0 bitcast_dynamic-update-slice_fusion.5
  174.3 0.7 bitcast_dynamic-update-slice_fusion.21
  175.1 1.1 pad_maximum_fusion.2
  176.3 1.1 copy-done
  177.5 1.9 subtract_dynamic-update-slice_fusion
  179.5 0.9 bitcast_dynamic-update-slice_fusion.14
  180.4 0.9 fusion.108
  181.6 0.3 fusion.120
  182.0 1.5 pad_maximum_fusion
  183.6 1.1 fusion.155
  184.9 1.1 fusion.28
  187.0 0.3 fusion.50
  187.6 0.3 fusion.24
  188.0 2.4 multiply_reduce_fusion.13
  190.4 1.4 fusion.177
  192.4 0.7 broadcast_multiply_fusion
  193.1 0.7 broadcast_multiply_fusion.1
  193.9 0.8 fusion.1
  194.7 1.9 collective-permute-start.2
  196.6 2.6 collective-permute-start.3
  199.2 0.8 fusion.134
  200.0 1.7 gather_fusion
  201.8 1.1 fusion.140
  202.8 1.0 fusion.146
  203.9 4.4 %collective-permute-done.3 = f32[2,1,256,128]{3,2,1,0:T(8,128)} collective-permute-done((f32[2,1,256,128]{3,2,1,0:T(8,128)}, f32[2,1,256,128]{3,2,1,0:T(8,128)}, u32[]{:S(2)}, u32[]{:S(2)}) %collective-permute-start.3) | collective-permute-done | bytes 262176 | tf_op jit(solution)/shard_map/ppermute | solution.py:14
  208.3 1.1 pad_maximum_fusion.1
  209.5 1.2 fusion.152
  211.4 0.3 fusion.98
  212.5 0.3 fusion.72
  212.8 0.5 copy-done.8
  213.4 0.5 copy-done.10
  213.8 5.6 %multiply_reduce_fusion.2 = (f32[2,256,128]{2,1,0:T(8,128)}, f32[2,256,128]{2,1,0:T(8,128)}, f32[2,256,128]{2,1,0:T(8,128)}, f32[2,256,128]{2,1,0:T(8,128)}, f32...) fusion(f32[6,2,256,128]{3,2,1,0:T(8,128)} %bitcast_dynamic-upda, ...), kind=kLoop, calls=%fused_computation.101 | loop fusion | flops 8650752 | bytes 17301504 | tf_op jit(solution)/shard_map/reduce_sum | solution.py:110
  219.4 2.2 fusion.182
  221.8 1.7 gather_fusion.1
  223.5 42.5 %all-gather.1 = f32[32,2,256]{2,1,0:T(2,128)S(1)} all-gather(f32[1,2,256]{2,1,0:T(2,128)S(1)} %maximum_bitcast_fusion), channel_id=2, replica_groups=mesh['shot'=8,'domain'=32] {'domain'}, dimensions={0}, use_global_device_ids=true | all-gather | bytes 67584 | tf_op jit(solution)/shard_map/all_gather | solution.py:210
  266.1 2.1 fusion.160
  268.2 2.4 scatter_fusion
  270.7 2.0 bitcast_dynamic-update-slice_fusion.13
  272.7 0.8 bitcast_dynamic-update-slice_fusion.12
  273.5 0.9 bitcast_dynamic-update-slice_fusion.11
  274.7 1.0 bitcast_dynamic-update-slice_fusion.4
  276.0 1.0 bitcast_dynamic-update-slice_fusion
  277.0 44.3 %reduce-scatter.2.cloned.1.call-done = f32[5,2,32,128]{3,2,1,0:T(8,128)} async-done(((f32[5,2,256,128]{3,2,1,0:T(8,128)}), f32[5,2,32,128]{3,2,1,0:T(8,128)}) %reduce-scatter.2.cloned.1.call-update) | async-done | bytes 163856 | tf_op jit(solution)/shard_map/reduce_scatter | solution.py:226
  (119 shorter events, 5.2 us)
Async XLA Ops:
  6.5 6.3 %copy-start.1 = (f32[1,4,2,256,128]{4,3,2,1,0:T(8,128)S(1)}, f32[1,4,2,256,128]{4,3,2,1,0:T(8,128)}, u32[]{:S(2)}) copy-start(f32[1,4,2,256,128]{4,3,2,1,0:T(8,128)} %param.22) | copy-start | bytes 3145732
  6.5 314.7 %reduce-scatter.2.cloned.1.call-start = ((), (), s32[]{:S(2)}) async-start(), calls=%async_computation.1 | async-start | bytes 1474560 | tf_op jit(solution)/shard_map/reduce_scatter | solution.py:226
  7.7 167.3 %copy-start.11 = (f32[1,2,256,128]{3,2,1,0:T(8,128)}, f32[1,2,256,128]{3,2,1,0:T(8,128)S(1)}, u32[]{:S(2)}) copy-start(f32[1,2,256,128]{3,2,1,0:T(8,128)S(1)} %get-tuple-element.73) | copy-start | bytes 786436
  7.7 167.3 %copy-start.14 = (f32[1,2,256,128]{3,2,1,0:T(8,128)}, f32[1,2,256,128]{3,2,1,0:T(8,128)S(1)}, u32[]{:S(2)}) copy-start(f32[1,2,256,128]{3,2,1,0:T(8,128)S(1)} %get-tuple-element.74) | copy-start | bytes 786436
  7.7 13.5 %copy-start.35 = (f32[2,32,128]{2,1,0:T(8,128)S(1)}, f32[2,32,128]{2,1,0:T(8,128)}, u32[]{:S(2)}) copy-start(f32[2,32,128]{2,1,0:T(8,128)} %param.20) | copy-start | bytes 98308
  8.5 166.6 %collective-permute-start.4 = (f32[2,1,256,128]{3,2,1,0:T(8,128)}, f32[2,1,256,128]{3,2,1,0:T(8,128)}, u32[]{:S(2)}, u32[]{:S(2)}) collective-permute-start(f32[2,1,256,128]{3,2,1,0:T(8,128)} %get-tuple-element.91), channel_id=1, source_target_pairs={{1,0},{2,1},{3,2},{4,3},{5,4},{6,5},{7,6},{8,7},{9,8},{10,9},{11,1... | collective-permute-start | bytes 786440 | tf_op jit(solution)/shard_map/ppermute | solution.py:17
  10.4 40.3 %copy-start.36 = (f32[2,32,128]{2,1,0:T(8,128)S(1)}, f32[2,32,128]{2,1,0:T(8,128)}, u32[]{:S(2)}) copy-start(f32[2,32,128]{2,1,0:T(8,128)} %param.21) | copy-start | bytes 98308
  10.4 164.7 %collective-permute-start.5 = (f32[2,1,256,128]{3,2,1,0:T(8,128)S(1)}, f32[2,1,256,128]{3,2,1,0:T(8,128)}, u32[]{:S(2)}, u32[]{:S(2)}) collective-permute-start(f32[2,1,256,128]{3,2,1,0:T(8,128)S(1)} %get-tuple-element.92), channel_id=1, source_target_pairs={{0,1},{1,2},{2,3},{3,4},{4,5},{5,6},{6,7},{7,8},{8,9},{9,10},{10,1... | collective-permute-start | bytes 786440 | tf_op jit(solution)/shard_map/ppermute | solution.py:14
  12.9 67.3 %copy-start.5 = (f32[1,2,256,128]{3,2,1,0:T(8,128)}, f32[1,2,256,128]{3,2,1,0:T(8,128)S(1)}, u32[]{:S(2)}) copy-start(f32[1,2,256,128]{3,2,1,0:T(8,128)S(1)} %get-tuple-element.86) | copy-start | bytes 786436
  12.9 171.9 %copy-start.3 = (f32[1,2,256,128]{3,2,1,0:T(8,128)}, f32[1,2,256,128]{3,2,1,0:T(8,128)S(1)}, u32[]{:S(2)}) copy-start(f32[1,2,256,128]{3,2,1,0:T(8,128)S(1)} %get-tuple-element.85) | copy-start | bytes 786436
  12.9 67.3 %copy-start.37 = (f32[2,32,128]{2,1,0:T(8,128)S(1)}, f32[2,32,128]{2,1,0:T(8,128)}, u32[]{:S(2)}) copy-start(f32[2,32,128]{2,1,0:T(8,128)} %param.17) | copy-start | bytes 98308
  12.9 95.7 %copy-start.38 = (f32[2,32,128]{2,1,0:T(8,128)S(1)}, f32[2,32,128]{2,1,0:T(8,128)}, u32[]{:S(2)}) copy-start(f32[2,32,128]{2,1,0:T(8,128)} %param.19) | copy-start | bytes 98308
  13.7 123.3 %copy-start.39 = (f32[2,32,128]{2,1,0:T(8,128)S(1)}, f32[2,32,128]{2,1,0:T(8,128)}, u32[]{:S(2)}) copy-start(f32[2,32,128]{2,1,0:T(8,128)} %param.18) | copy-start | bytes 98308
  13.7 151.6 %copy-start.41 = (f32[1,2]{1,0:T(1,128)S(1)}, f32[1,2]{1,0:T(1,128)}, u32[]{:S(2)}) copy-start(f32[1,2]{1,0:T(1,128)} %param.24) | copy-start | bytes 28
  13.7 168.3 %collective-permute-start = (f32[2,1,256,128]{3,2,1,0:T(8,128)}, f32[2,1,256,128]{3,2,1,0:T(8,128)}, u32[]{:S(2)}, u32[]{:S(2)}) collective-permute-start(f32[2,1,256,128]{3,2,1,0:T(8,128)} %get-tuple-element.99), channel_id=1, source_target_pairs={{1,0},{2,1},{3,2},{4,3},{5,4},{6,5},{7,6},{8,7},{9,8},{10,9},{11,1... | collective-permute-start | bytes 786440 | tf_op jit(solution)/shard_map/ppermute | solution.py:17
  18.5 163.5 %collective-permute-start.1 = (f32[2,1,256,128]{3,2,1,0:T(8,128)}, f32[2,1,256,128]{3,2,1,0:T(8,128)}, u32[]{:S(2)}, u32[]{:S(2)}) collective-permute-start(f32[2,1,256,128]{3,2,1,0:T(8,128)} %get-tuple-element.100), channel_id=1, source_target_pairs={{0,1},{1,2},{2,3},{3,4},{4,5},{5,6},{6,7},{7,8},{8,9},{9,10},{10,1... | collective-permute-start | bytes 786440 | tf_op jit(solution)/shard_map/ppermute | solution.py:14
  169.5 1.8 copy-start.40
  176.2 1.2 copy-start
  176.2 1.3 copy-start.12
  176.2 1.3 copy-start.15
  180.4 1.6 copy-start.6
  182.0 1.6 copy-start.25
  183.5 1.4 copy-start.2
  187.3 3.1 copy-start.9
  188.0 2.4 copy-start.7
  188.0 2.4 copy-start.4
  190.4 1.4 copy-start.16
  191.8 2.1 copy-start.18
  194.7 9.2 %collective-permute-start.2 = (f32[2,1,256,128]{3,2,1,0:T(8,128)}, f32[2,1,256,128]{3,2,1,0:T(8,128)}, u32[]{:S(2)}, u32[]{:S(2)}) collective-permute-start(f32[2,1,256,128]{3,2,1,0:T(8,128)} %get-tuple-element.97), channel_id=1, source_target_pairs={{1,0},{2,1},{3,2},{4,3},{5,4},{6,5},{7,6},{8,7},{9,8},{10,9},{11,1... | collective-permute-start | bytes 786440 | tf_op jit(solution)/shard_map/ppermute | solution.py:17
  196.6 11.7 %collective-permute-start.3 = (f32[2,1,256,128]{3,2,1,0:T(8,128)}, f32[2,1,256,128]{3,2,1,0:T(8,128)}, u32[]{:S(2)}, u32[]{:S(2)}) collective-permute-start(f32[2,1,256,128]{3,2,1,0:T(8,128)} %get-tuple-element.98), channel_id=1, source_target_pairs={{0,1},{1,2},{2,3},{3,4},{4,5},{5,6},{6,7},{7,8},{8,9},{9,10},{10,1... | collective-permute-start | bytes 786440 | tf_op jit(solution)/shard_map/ppermute | solution.py:14
  209.4 1.2 copy-start.24
  210.7 1.0 copy-start.22
  211.4 1.4 copy-start.26
  211.8 1.6 copy-start.8
  211.8 2.0 copy-start.10
  219.4 2.2 copy-start.20
  219.4 46.7 %copy-start.42 = (f32[1,2,256]{2,1,0:T(2,128)S(1)}, f32[1,2,256]{2,1,0:T(2,128)}, u32[]{:S(2)}) copy-start(f32[1,2,256]{2,1,0:T(2,128)} %param.27) | copy-start | bytes 6148
  219.4 46.7 %copy-start.13 = (f32[1,2,256,128]{3,2,1,0:T(8,128)S(1)}, f32[1,2,256,128]{3,2,1,0:T(8,128)}, u32[]{:S(2)}) copy-start(f32[1,2,256,128]{3,2,1,0:T(8,128)} %copy-done.11) | copy-start | bytes 786436
  268.2 2.4 copy-start.17
  268.2 2.4 copy-start.19
  268.2 2.4 copy-start.21
  268.2 2.4 copy-start.23
  273.4 0.9 copy-start.31
  273.4 1.0 copy-start.32
  273.4 1.2 copy-start.33
  273.5 1.3 copy-start.34
  274.7 1.0 copy-start.27
  274.7 1.0 copy-start.28
  274.7 1.1 copy-start.29
  274.7 1.3 copy-start.30
Sparse Core Ops, SparseCore 0:
  277.1 44.0 reduce-scatter.1
